TPU v7x, 32 devices: a whole 2x2x4 slice. The times are simulated.
32 devices in a mesh: dp: 8 (over z, y), fsdp: 4 (over x, core).
Axes of the slice: x: 2, y: 2, z: 4, core: 2. Of those that a mesh axis runs over, the one named last changes fastest.
Arguments:
- tokens: bfloat16 [64, 512, 1024], P(('dp', 'fsdp')), may hold values from -6 to 6
- cotangent: bfloat16 [64, 512, 1024], P(('dp', 'fsdp')), may hold values from -6 to 6
- adapter_id: int32 [64], P(('dp', 'fsdp')), may hold values from 0 to 7
- global_pos: int32 [64, 64], P(('dp', 'fsdp')), may hold values from 0 to 511, as said below
- w_qkv: bfloat16 [1024, 3072], P(('dp', 'fsdp')), may hold values from -0.1875 to 0.1875
- w_out: bfloat16 [1024, 1024], P(('dp', 'fsdp')), may hold values from -0.75 to 0.75
- w_up: bfloat16 [1024, 4096], P(('dp', 'fsdp')), may hold values from -0.1875 to 0.1875
- w_down: bfloat16 [4096, 1024], P(('dp', 'fsdp')), may hold values from -0.09375 to 0.09375
- norm_gain: bfloat16 [1024, 2], P(('dp', 'fsdp')), may hold values from 0.5 to 1.5
- norm_bias: bfloat16 [1024, 2], P(('dp', 'fsdp')), may hold values from -3 to 3
- narrow_in: bfloat16 [1024, 640], P(('dp', 'fsdp')), may hold values from -0.1875 to 0.1875
- widen_out: bfloat16 [1024, 640], P(('dp', 'fsdp')), may hold values from -0.75 to 0.75
- ff_narrow: bfloat16 [4096, 128], P(('dp', 'fsdp')), may hold values from -0.09375 to 0.09375
- ff_widen: bfloat16 [4096, 128], P(('dp', 'fsdp')), may hold values from -0.75 to 0.75
Outputs:
- output: bfloat16 [64, 512, 1024], P(('dp', 'fsdp'))
- input_grad: bfloat16 [64, 512, 1024], P(('dp', 'fsdp'))
- narrow_in_grad: float32 [1024, 640], P(('dp', 'fsdp'))
- widen_out_grad: float32 [1024, 640], P(('dp', 'fsdp'))
- ff_narrow_grad: float32 [4096, 128], P(('dp', 'fsdp'))
- ff_widen_grad: float32 [4096, 128], P(('dp', 'fsdp'))
Inputs may be any that keep to these rules, and one draw needn't show every extreme that they name: `global_pos`: the 64 positions in each sequence's row are distinct.
All inputs are finite; a program needn't handle non-finite values.
Results may differ from a plain program's by a relative error of at most 0.015.
The roundings to bfloat16 on the way count: a program that leaves them out, or rounds other values in their place, can miss the bound.
Values may be sent and summed in bfloat16 or wider, within the bound.
A program may use at most 192 MiB of HBM per device.

v0:
```python
import jax
import jax.numpy as jnp
from jax import lax
from jax.sharding import PartitionSpec as P

HEAD_DIM = 64
SETS = 8
R = 16
WINDOW = 512


def normalize(values, gain, shift):
    center = values - jnp.mean(values, axis=-1, keepdims=True)
    spread = jnp.mean(center * center, axis=-1, keepdims=True)
    return center * lax.rsqrt(spread + 1e-12) * gain + shift


def against(left, right):
    return lax.dot_general(
        left, right, (((1,), (1,)), ((), ())), preferred_element_type=jnp.float32
    )


def over_rows(left, right):
    return lax.dot_general(
        left, right, (((0,), (0,)), ((), ())), preferred_element_type=jnp.float32
    )


def product(left, right):
    return jnp.dot(left, right, preferred_element_type=jnp.float32)


def gelu_exact(values):
    return jax.nn.gelu(values, approximate=False)


def local(
    tokens,
    cotangent,
    adapter_id,
    global_pos,
    w_qkv,
    w_out,
    w_up,
    w_down,
    norm_gain,
    norm_bias,
    narrow_in,
    widen_out,
    ff_narrow,
    ff_widen,
):
    gathered = (
        lax.all_gather(w_qkv, ("dp", "fsdp"), axis=0, tiled=True),
        lax.all_gather(w_out, ("dp", "fsdp"), axis=0, tiled=True),
        lax.all_gather(w_up, ("dp", "fsdp"), axis=0, tiled=True),
        lax.all_gather(w_down, ("dp", "fsdp"), axis=0, tiled=True),
        lax.all_gather(norm_gain, ("dp", "fsdp"), axis=0, tiled=True),
        lax.all_gather(norm_bias, ("dp", "fsdp"), axis=0, tiled=True),
        lax.all_gather(narrow_in, ("dp", "fsdp"), axis=0, tiled=True),
        lax.all_gather(widen_out, ("dp", "fsdp"), axis=0, tiled=True),
        lax.all_gather(ff_narrow, ("dp", "fsdp"), axis=0, tiled=True),
        lax.all_gather(ff_widen, ("dp", "fsdp"), axis=0, tiled=True),
    )
    (
        wq_full,
        wo_full,
        wu_full,
        wd_full,
        gain_full,
        shift_full,
        a_full,
        b_full,
        ffa_full,
        ffb_full,
    ) = gathered
    seq_local, length, model_width = tokens.shape
    rows_all = seq_local * length
    heads = model_width // HEAD_DIM
    set_cols = SETS * R
    scale = HEAD_DIM ** (-0.5)
    chosen = (
        lax.broadcasted_iota(jnp.int32, (seq_local, set_cols), 1) // R == adapter_id[:, None]
    ).astype(jnp.float32)
    chosen = jnp.broadcast_to(chosen[:, None, :], (seq_local, length, set_cols)).reshape(
        rows_all, set_cols
    )
    chosen_three = jnp.concatenate([chosen, chosen, chosen], axis=1)
    positions = lax.broadcasted_iota(jnp.int32, (length,), 0)
    nearby = jnp.abs(positions[:, None] - positions[None, :]) <= WINDOW // 2
    is_global = jnp.any(global_pos[:, :, None] == positions[None, None, :], axis=1)
    gain_one = gain_full[:, 0].astype(jnp.float32)
    gain_two = gain_full[:, 1].astype(jnp.float32)
    shift_one = shift_full[:, 0].astype(jnp.float32)
    shift_two = shift_full[:, 1].astype(jnp.float32)

    def cols_of(slot):
        return slice(slot * set_cols, (slot + 1) * set_cols)

    flat_in = tokens.reshape(rows_all, model_width)
    qkv_main = product(flat_in, wq_full)
    t_qkv = (product(flat_in, a_full[:, : 3 * set_cols]) * chosen_three).astype(jnp.bfloat16)
    projected = []
    for slot in range(3):
        summed = qkv_main[:, slot * model_width : (slot + 1) * model_width] + against(
            t_qkv[:, cols_of(slot)], b_full[:, cols_of(slot)]
        )
        projected.append(summed.astype(jnp.bfloat16))
    query_low, key_low, value_low = projected
    query_heads = query_low.reshape(seq_local, length, heads, HEAD_DIM)
    key_heads = key_low.reshape(seq_local, length, heads, HEAD_DIM)
    value_heads = value_low.reshape(seq_local, length, heads, HEAD_DIM)

    def scores_of(query_one, key_one, glob_one):
        allowed = nearby | glob_one[None, :] | glob_one[:, None]
        scores = (
            jnp.einsum("qhd,khd->hqk", query_one, key_one, preferred_element_type=jnp.float32)
            * scale
        )
        return jnp.where(allowed[None], scores, -1e30)

    def attend(items):
        query_one, key_one, value_one, glob_one = items
        scores = scores_of(query_one, key_one, glob_one)
        row_top = jnp.max(scores, axis=-1, keepdims=True)
        shifted = jnp.exp(scores - row_top)
        row_total = jnp.sum(shifted, axis=-1, keepdims=True)
        weights_low = (shifted / row_total).astype(jnp.bfloat16)
        mixed_one = jnp.einsum(
            "hqk,khd->qhd", weights_low, value_one, preferred_element_type=jnp.float32
        )
        return (
            mixed_one.reshape(length, model_width).astype(jnp.bfloat16),
            (row_top + jnp.log(row_total))[..., 0],
        )

    mixed_low, log_total = lax.map(attend, (query_heads, key_heads, value_heads, is_global))
    mixed_flat = mixed_low.reshape(rows_all, model_width)
    t_out = (product(mixed_flat, a_full[:, cols_of(3)]) * chosen).astype(jnp.bfloat16)
    attn_out = product(mixed_flat, wo_full) + against(t_out, b_full[:, cols_of(3)])
    resid = flat_in.astype(jnp.float32) + attn_out
    normed, norm_one_back = jax.vjp(lambda values: normalize(values, gain_one, shift_one), resid)
    normed_low = normed.astype(jnp.bfloat16)
    t_up = (product(normed_low, a_full[:, cols_of(4)]) * chosen).astype(jnp.bfloat16)
    pre_act = product(normed_low, wu_full) + against(t_up, ffb_full)
    activation, gelu_back = jax.vjp(gelu_exact, pre_act)
    act_low = activation.astype(jnp.bfloat16)
    t_down = (product(act_low, ffa_full) * chosen).astype(jnp.bfloat16)
    down_out = product(act_low, wd_full) + against(t_down, b_full[:, cols_of(4)])
    final = normed + down_out
    result, norm_two_back = jax.vjp(lambda values: normalize(values, gain_two, shift_two), final)
    regathered = (
        lax.all_gather(w_qkv, ("dp", "fsdp"), axis=0, tiled=True),
        lax.all_gather(w_out, ("dp", "fsdp"), axis=0, tiled=True),
        lax.all_gather(w_up, ("dp", "fsdp"), axis=0, tiled=True),
        lax.all_gather(w_down, ("dp", "fsdp"), axis=0, tiled=True),
        lax.all_gather(norm_gain, ("dp", "fsdp"), axis=0, tiled=True),
        lax.all_gather(norm_bias, ("dp", "fsdp"), axis=0, tiled=True),
        lax.all_gather(narrow_in, ("dp", "fsdp"), axis=0, tiled=True),
        lax.all_gather(widen_out, ("dp", "fsdp"), axis=0, tiled=True),
        lax.all_gather(ff_narrow, ("dp", "fsdp"), axis=0, tiled=True),
        lax.all_gather(ff_widen, ("dp", "fsdp"), axis=0, tiled=True),
    )
    (
        wq_full,
        wo_full,
        wu_full,
        wd_full,
        gain_full,
        shift_full,
        a_full,
        b_full,
        ffa_full,
        ffb_full,
    ) = regathered
    d_final = norm_two_back(cotangent.reshape(rows_all, model_width).astype(jnp.float32))[0]
    d_down = d_final.astype(jnp.bfloat16)
    dt_down = (product(d_down, b_full[:, cols_of(4)]) * chosen).astype(jnp.bfloat16)
    grad_b_down = over_rows(d_down, t_down)
    grad_ff_narrow = over_rows(act_low, dt_down)
    d_act = against(d_down, wd_full) + against(dt_down, ffa_full)
    d_pre = gelu_back(d_act)[0].astype(jnp.bfloat16)
    dt_up = (product(d_pre, ffb_full) * chosen).astype(jnp.bfloat16)
    grad_ff_widen = over_rows(d_pre, t_up)
    grad_a_up = over_rows(normed_low, dt_up)
    d_normed = d_final + against(d_pre, wu_full) + against(dt_up, a_full[:, cols_of(4)])
    d_resid = norm_one_back(d_normed)[0]
    d_attn = d_resid.astype(jnp.bfloat16)
    dt_out = (product(d_attn, b_full[:, cols_of(3)]) * chosen).astype(jnp.bfloat16)
    grad_b_out = over_rows(d_attn, t_out)
    grad_a_out = over_rows(mixed_flat, dt_out)
    d_mixed = (against(d_attn, wo_full) + against(dt_out, a_full[:, cols_of(3)])).astype(
        jnp.bfloat16
    )
    d_mixed_heads = d_mixed.reshape(seq_local, length, heads, HEAD_DIM)

    def attend_back(items):
        query_one, key_one, value_one, glob_one, total_one, d_one = items
        scores = scores_of(query_one, key_one, glob_one)
        weights_full = jnp.exp(scores - total_one[..., None])
        weights_low = weights_full.astype(jnp.bfloat16)
        d_value = jnp.einsum("hqk,qhd->khd", weights_low, d_one, preferred_element_type=jnp.float32)
        d_weights = jnp.einsum("qhd,khd->hqk", d_one, value_one, preferred_element_type=jnp.float32)
        inner = jnp.sum(weights_full * d_weights, axis=-1, keepdims=True)
        d_scores = (weights_full * (d_weights - inner)).astype(jnp.bfloat16)
        d_query = (
            jnp.einsum("hqk,khd->qhd", d_scores, key_one, preferred_element_type=jnp.float32)
            * scale
        )
        d_key = (
            jnp.einsum("hqk,qhd->khd", d_scores, query_one, preferred_element_type=jnp.float32)
            * scale
        )
        return (
            d_query.reshape(length, model_width).astype(jnp.bfloat16),
            d_key.reshape(length, model_width).astype(jnp.bfloat16),
            d_value.reshape(length, model_width).astype(jnp.bfloat16),
        )

    d_query_all, d_key_all, d_value_all = lax.map(
        attend_back, (query_heads, key_heads, value_heads, is_global, log_total, d_mixed_heads)
    )
    d_parts = [
        d_query_all.reshape(rows_all, model_width),
        d_key_all.reshape(rows_all, model_width),
        d_value_all.reshape(rows_all, model_width),
    ]
    d_qkv = jnp.concatenate(d_parts, axis=1)
    dt_qkv = (
        jnp.concatenate(
            [product(d_parts[slot], b_full[:, cols_of(slot)]) for slot in range(3)], axis=1
        )
        * chosen_three
    ).astype(jnp.bfloat16)
    grad_b_qkv = [over_rows(d_parts[slot], t_qkv[:, cols_of(slot)]) for slot in range(3)]
    grad_a_qkv = over_rows(flat_in, dt_qkv)
    d_input = d_resid + against(d_qkv, wq_full) + against(dt_qkv, a_full[:, : 3 * set_cols])
    grad_narrow = jnp.concatenate([grad_a_qkv, grad_a_out, grad_a_up], axis=1)
    grad_widen = jnp.concatenate(grad_b_qkv + [grad_b_out, grad_b_down], axis=1)
    sums = (
        lax.psum_scatter(grad_narrow, ("dp", "fsdp"), scatter_dimension=0, tiled=True),
        lax.psum_scatter(grad_widen, ("dp", "fsdp"), scatter_dimension=0, tiled=True),
        lax.psum_scatter(grad_ff_narrow, ("dp", "fsdp"), scatter_dimension=0, tiled=True),
        lax.psum_scatter(grad_ff_widen, ("dp", "fsdp"), scatter_dimension=0, tiled=True),
    )
    return (
        result.reshape(seq_local, length, model_width).astype(jnp.bfloat16),
        d_input.reshape(seq_local, length, model_width).astype(jnp.bfloat16),
        sums[0],
        sums[1],
        sums[2],
        sums[3],
    )


def solution(mesh):
    in_specs = (
        P(("dp", "fsdp"), None, None),
        P(("dp", "fsdp"), None, None),
        P(("dp", "fsdp")),
        P(("dp", "fsdp"), None),
        P(("dp", "fsdp"), None),
        P(("dp", "fsdp"), None),
        P(("dp", "fsdp"), None),
        P(("dp", "fsdp"), None),
        P(("dp", "fsdp"), None),
        P(("dp", "fsdp"), None),
        P(("dp", "fsdp"), None),
        P(("dp", "fsdp"), None),
        P(("dp", "fsdp"), None),
        P(("dp", "fsdp"), None),
    )
    out_specs = (
        P(("dp", "fsdp"), None, None),
        P(("dp", "fsdp"), None, None),
        P(("dp", "fsdp"), None),
        P(("dp", "fsdp"), None),
        P(("dp", "fsdp"), None),
        P(("dp", "fsdp"), None),
    )
    return jax.shard_map(local, mesh=mesh, in_specs=in_specs, out_specs=out_specs, check_vma=False)
```

profile of v0, /device:TPU:0, one launch (start us, length us, event | category | flops | bytes accessed | tf_op | source)
XLA Modules:
  0.0 1097.7 jit_solution(15863523064765116602)
XLA Ops:
  13.5 43.5 %all-gather = bf16[32,32,2]{1,2,0:T(2,128)(2,1)S(1)} all-gather(bf16[1,32,2]{1,2,0:T(2,128)(2,1)} %bitcast.220), channel_id=1, replica_groups=mesh['dp'=8,'fsdp'=4] {'dp','fsdp'}, dimensions={0}, use_global_device_ids=true | all-gather | bytes 4224 | tf_op jit(solution)/shard_map/all_gather | solution.py:59
  57.7 36.8 %all-gather.1 = bf16[32,32,2]{1,2,0:T(2,128)(2,1)S(1)} all-gather(bf16[1,32,2]{1,2,0:T(2,128)(2,1)} %bitcast.221), channel_id=1, replica_groups=mesh['dp'=8,'fsdp'=4] {'dp','fsdp'}, dimensions={0}, use_global_device_ids=true | all-gather | bytes 4224 | tf_op jit(solution)/shard_map/all_gather | solution.py:60
  99.8 39.0 %all-gather.11.cloned.1.call-done = bf16[1024,3072]{1,0:T(8,128)(2,1)} async-done(((bf16[32,3072]{1,0:T(8,128)(2,1)}), bf16[1024,3072]{1,0:T(8,128)(2,1)}) %all-gather.11.cloned.1.call-update) | async-done | bytes 6291472 | tf_op jit(solution)/shard_map/all_gather | solution.py:55
  138.8 12.4 %fusion.113 = f32[1024,3072]{1,0:T(8,128)} fusion(bf16[1024,1024]{1,0:T(8,128)(2,1)S(1)} %bitcast.204, bf16[1024,3072]{1,0:T(8,128)(2,1)} %all-gather.11.cloned.1.call-done), kind=kOutput, calls=%fused_computation.187 | convolution fusion | flops 6442450944 | bytes 20971520 | tf_op jit(solution)/shard_map/dot_general | solution.py:31
  151.2 43.3 %all-gather.15.cloned.1.call-done = bf16[1024,640]{1,0:T(8,128)(2,1)} async-done(((bf16[32,640]{1,0:T(8,128)(2,1)}), bf16[1024,640]{1,0:T(8,128)(2,1)}) %all-gather.15.cloned.1.call-update) | async-done | bytes 1310736 | tf_op jit(solution)/shard_map/all_gather | solution.py:62
  232.4 60.1 %while.28 = (s32[]{:T(128)}, bf16[2,512,1024]{2,1,0:T(8,128)(2,1)}, f32[2,16,512]{2,1,0:T(8,128)S(1)}, bf16[2,512,16,64]{1,3,2,0:T(8,128)(2,1)}, pred[2,512]{1,0...) while((s32[]{:T(128)}, bf16[2,512,1024]{2,1,0:T(8,128)(2,1)}, ...), condition=%wide.region_4.5_spmd.clone, body=%wide.region_1.4_spmd.clone.sunk | while | flops 1125900288 | bytes 60034652 | solution.py:138
  306.2 24.8 %all-gather.19.cloned.1.call-done = bf16[1024,4096]{1,0:T(8,128)(2,1)} async-done(((bf16[32,4096]{1,0:T(8,128)(2,1)}), bf16[1024,4096]{1,0:T(8,128)(2,1)}) %all-gather.19.cloned.1.call-update) | async-done | bytes 8388624 | tf_op jit(solution)/shard_map/all_gather | solution.py:57
  331.0 14.5 %fusion.115 = f32[1024,4096]{1,0:T(8,128)} fusion(bf16[1024,1024]{1,0:T(8,128)(2,1)S(1)} %fusion.66, bf16[1024,4096]{1,0:T(8,128)(2,1)} %all-gather.19.cloned.1.call-done), kind=kOutput, calls=%fused_computation.189 | convolution fusion | flops 8589934592 | bytes 27262976 | tf_op jit(solution)/shard_map/dot_general | solution.py:31
  345.4 40.5 %all-gather.21.cloned.1.call-done = bf16[4096,128]{1,0:T(8,128)(2,1)} async-done(((bf16[128,128]{1,0:T(8,128)(2,1)}), bf16[4096,128]{1,0:T(8,128)(2,1)}) %all-gather.21.cloned.1.call-update) | async-done | bytes 1048592 | tf_op jit(solution)/shard_map/all_gather | solution.py:64
  385.9 41.7 %multiply_convert_fusion.3 = (bf16[1024,4096]{1,0:T(8,128)(2,1)}, f32[1024,4096]{1,0:T(8,128)}, f32[1024,4096]{1,0:T(8,128)}) fusion(f32[1024,4096]{1,0:T(8,128)} %fusion.115, bf16[1024,128]{1,0:T(8,128)(2,1)S(1)} %fusion.74, bf16[4096,128]{1,0:T(8,128)(2,1)} %all-gather.21.cloned.1.call-done), kind=kOutput, calls=%fused_computation.65 | convolution fusion | flops 1350565888 | bytes 60030976 | tf_op jit(solution)/shard_map/dot_general | solution.py:19
  427.6 37.2 %all-gather.23.cloned.1.call-done = bf16[4096,1024]{1,0:T(8,128)(2,1)} async-done(((bf16[128,1024]{1,0:T(8,128)(2,1)}), bf16[4096,1024]{1,0:T(8,128)(2,1)}) %all-gather.23.cloned.1.call-update) | async-done | bytes 8388624 | tf_op jit(solution)/shard_map/all_gather | solution.py:58
  464.9 15.1 %fusion.116 = f32[1024,1024]{1,0:T(8,128)} fusion(bf16[1024,4096]{1,0:T(8,128)(2,1)} %get-tuple-element.283, bf16[4096,1024]{1,0:T(8,128)(2,1)} %all-gather.23.cloned.1.call-done), kind=kOutput, calls=%fused_computation.190 | convolution fusion | flops 8589934592 | bytes 20971520 | tf_op jit(solution)/shard_map/dot_general | solution.py:31
  479.9 40.1 %all-gather.25.cloned.1.call-done = bf16[4096,128]{1,0:T(8,128)(2,1)} async-done(((bf16[128,128]{1,0:T(8,128)(2,1)}), bf16[4096,128]{1,0:T(8,128)(2,1)}) %all-gather.25.cloned.1.call-update) | async-done | bytes 1048592 | tf_op jit(solution)/shard_map/all_gather | solution.py:63
  539.4 14.7 %fusion.117 = f32[1024,4096]{1,0:T(8,128)} fusion(bf16[1024,1024]{1,0:T(8,128)(2,1)S(1)} %add_convert_fusion.5, bf16[4096,1024]{1,0:T(8,128)(2,1)} %all-gather.23.cloned.1.call-done), kind=kOutput, calls=%fused_computation.191 | convolution fusion | flops 8589934592 | bytes 27262976 | tf_op jit(solution)/shard_map/dot_general | solution.py:19
  554.2 22.0 %add_convert_fusion = bf16[1024,4096]{1,0:T(8,128)(2,1)} fusion(f32[1024,4096]{1,0:T(8,128)} %get-tuple-element.284, f32[1024,4096]{1,0:T(8,128)} %fusion.117, f32[1024,4096]{1,0:T(8,128)} %get-tuple-element.300, bf16[1024,128]{1,0:T(8,128)(2,1)S(1)} %copy-done.55, bf16[4096,128]{1,0:T(8,128)(2,1)S(1)} %copy-done.51), kind=kOutput, calls=%fused_computation.64 | convolution fusion | flops 1136656384 | bytes 60030976 | tf_op jit(solution)/shard_map/dot_general | solution.py:19
  576.1 13.0 %fusion.118 = f32[1024,1024]{1,0:T(8,128)S(1)} fusion(bf16[1024,4096]{1,0:T(8,128)(2,1)} %add_convert_fusion, bf16[1024,4096]{1,0:T(8,128)(2,1)} %all-gather.19.cloned.1.call-done), kind=kOutput, calls=%fused_computation.192 | convolution fusion | flops 8589934592 | bytes 20971520 | tf_op jit(solution)/shard_map/dot_general | solution.py:19
  625.9 125.4 %while.29 = (s32[]{:T(128)}, bf16[2,512,1024]{2,1,0:T(8,128)(2,1)}, bf16[2,512,1024]{2,1,0:T(8,128)(2,1)}, bf16[2,512,1024]{2,1,0:T(8,128)(2,1)}, bf16[2,512,16,...) while((s32[]{:T(128)}, bf16[2,512,1024]{2,1,0:T(8,128)(2,1)}, ...), condition=%wide.region_15.16_spmd.clone, body=%wide.region_13.15_spmd.clone.sunk | while | flops 2726027264 | bytes 191534256 | solution.py:221
  636.3 12.0 %multiply_reduce_fusion.5 = (f32[16,512]{1,0:T(8,128)S(1)}, f32[16,512,512]{1,2,0:T(8,128)}) fusion(f32[16,512,512]{1,2,0:T(8,128)} %fusion.206, f32[16,512]{1,0:T(8,128)S(1)} %dynamic-slice_bitcast_fusion.2, bf16[2,512,16,64]{1,3,2,0:T(8,128)(2,1)S(1)} %get-tuple-element.473, s32[]{:T(128)} %get-tuple-element.458, ...), kind=kOutput, calls=%fused_computation.27.clone.1 | convolution fusion | flops 557834240 | bytes 35980288 | tf_op jit(solution)/shard_map/while/body/eval_jaxpr/qhd,khd->hqk/dot_general | solution.py:118
  648.3 11.6 %multiply_convert_fusion.7 = bf16[16,512,512]{1,2,0:T(8,128)(2,1)S(1)} fusion(f32[16,512,512]{1,2,0:T(8,128)} %get-tuple-element.419, f32[16,512,512]{1,2,0:T(8,128)} %fusion.206, f32[16,512]{1,0:T(8,128)S(1)} %get-tuple-element.420), kind=kLoop, calls=%fused_computation.26.clone.1 | loop fusion | flops 12582912 | bytes 41975808 | tf_op jit(solution)/shard_map/while/body/eval_jaxpr/convert_element_type | solution.py:206
  698.8 12.0 %multiply_reduce_fusion.5 = (f32[16,512]{1,0:T(8,128)S(1)}, f32[16,512,512]{1,2,0:T(8,128)}) fusion(f32[16,512,512]{1,2,0:T(8,128)} %fusion.206, f32[16,512]{1,0:T(8,128)S(1)} %dynamic-slice_bitcast_fusion.2, bf16[2,512,16,64]{1,3,2,0:T(8,128)(2,1)S(1)} %get-tuple-element.473, s32[]{:T(128)} %get-tuple-element.458, ...), kind=kOutput, calls=%fused_computation.27.clone.1 | convolution fusion | flops 557834240 | bytes 35980288 | tf_op jit(solution)/shard_map/while/body/eval_jaxpr/qhd,khd->hqk/dot_general | solution.py:118
  710.8 11.6 %multiply_convert_fusion.7 = bf16[16,512,512]{1,2,0:T(8,128)(2,1)S(1)} fusion(f32[16,512,512]{1,2,0:T(8,128)} %get-tuple-element.419, f32[16,512,512]{1,2,0:T(8,128)} %fusion.206, f32[16,512]{1,0:T(8,128)S(1)} %get-tuple-element.420), kind=kLoop, calls=%fused_computation.26.clone.1 | loop fusion | flops 12582912 | bytes 41975808 | tf_op jit(solution)/shard_map/while/body/eval_jaxpr/convert_element_type | solution.py:206
  785.0 29.0 %reduce-scatter.11.cloned.1.call-done = f32[128,128]{1,0:T(8,128)} async-done(((f32[4096,128]{1,0:T(8,128)}), f32[128,128]{1,0:T(8,128)}) %reduce-scatter.11.cloned.1.call-update) | async-done | bytes 65552 | tf_op jit(solution)/shard_map/reduce_scatter | solution.py:245
  813.9 138.3 %reduce-scatter.15.cloned.1.call-done = f32[32,640]{1,0:T(8,128)} async-done(((f32[1024,640]{1,0:T(8,128)}), f32[32,640]{1,0:T(8,128)}) %reduce-scatter.15.cloned.1.call-update) | async-done | bytes 81936
  952.2 138.2 %reduce-scatter.13.cloned.1.call-done = f32[32,640]{1,0:T(8,128)} async-done(((f32[1024,640]{1,0:T(8,128)}), f32[32,640]{1,0:T(8,128)}) %reduce-scatter.13.cloned.1.call-update) | async-done | bytes 81936
  (304 shorter events, 289.6 us)
Async XLA Ops:
  7.2 88.8 %all-gather.13.cloned.1.call-start = ((), (), s32[]{:S(2)}) async-start(), calls=%async_computation.5 | async-start | bytes 1351680 | tf_op jit(solution)/shard_map/all_gather | solution.py:61
  7.9 130.9 %all-gather.11.cloned.1.call-start = ((), (), s32[]{:S(2)}) async-start(), calls=%async_computation.4 | async-start | bytes 6488064 | tf_op jit(solution)/shard_map/all_gather | solution.py:55
  8.6 185.8 %all-gather.15.cloned.1.call-start = ((), (), s32[]{:S(2)}) async-start(), calls=%async_computation.6 | async-start | bytes 1351680 | tf_op jit(solution)/shard_map/all_gather | solution.py:62
  9.4 286.3 %all-gather.17.cloned.1.call-start = ((), (), s32[]{:S(2)}) async-start(), calls=%async_computation.7 | async-start | bytes 2162688 | tf_op jit(solution)/shard_map/all_gather | solution.py:56
  10.0 321.0 %all-gather.19.cloned.1.call-start = ((), (), s32[]{:S(2)}) async-start(), calls=%async_computation.8 | async-start | bytes 8650752 | tf_op jit(solution)/shard_map/all_gather | solution.py:57
  10.5 128.2 %copy-start.38 = (bf16[2,512,1024]{2,1,0:T(8,128)(2,1)S(1)}, bf16[2,512,1024]{2,1,0:T(8,128)(2,1)}, u32[]{:S(2)}) copy-start(bf16[2,512,1024]{2,1,0:T(8,128)(2,1)} %param.18) | copy-start | bytes 6291460
  10.6 375.4 %all-gather.21.cloned.1.call-start = ((), (), s32[]{:S(2)}) async-start(), calls=%async_computation.9 | async-start | bytes 1081344 | tf_op jit(solution)/shard_map/all_gather | solution.py:64
  11.1 453.7 %all-gather.23.cloned.1.call-start = ((), (), s32[]{:S(2)}) async-start(), calls=%async_computation.10 | async-start | bytes 8650752 | tf_op jit(solution)/shard_map/all_gather | solution.py:58
  11.9 508.1 %all-gather.25.cloned.1.call-start = ((), (), s32[]{:S(2)}) async-start(), calls=%async_computation.11 | async-start | bytes 1081344 | tf_op jit(solution)/shard_map/all_gather | solution.py:63
  12.6 772.3 %reduce-scatter.9.cloned.1.call-start = ((), (), s32[]{:S(2)}) async-start(), calls=%async_computation.12 | async-start | bytes 2162688 | tf_op jit(solution)/shard_map/reduce_scatter | solution.py:244
  99.8 119.5 %copy-start.36 = (bf16[1024,384]{1,0:T(8,128)(2,1)}, bf16[1024,384]{1,0:T(8,128)(2,1)S(1)}, u32[]{:S(2)}) copy-start(bf16[1024,384]{1,0:T(8,128)(2,1)S(1)} %fusion.69) | copy-start | bytes 2359300
  232.4 60.2 %copy-start.63 = (f32[2,128]{1,0:T(2,128)S(1)}, f32[2,128]{1,0:T(2,128)}, u32[]{:S(2)}) copy-start(f32[2,128]{1,0:T(2,128)} %copy-done.62) | copy-start | bytes 3076
  304.3 41.1 %copy-start.12 = (bf16[1024,1024]{1,0:T(8,128)(2,1)}, bf16[1024,1024]{1,0:T(8,128)(2,1)S(1)}, u32[]{:S(2)}) copy-start(bf16[1024,1024]{1,0:T(8,128)(2,1)S(1)} %fusion.66) | copy-start | bytes 6291460
  306.2 79.8 %copy-start.52 = (bf16[1024,128]{1,0:T(8,128)(2,1)}, bf16[1024,128]{1,0:T(8,128)(2,1)S(1)}, u32[]{:S(2)}) copy-start(bf16[1024,128]{1,0:T(8,128)(2,1)S(1)} %fusion.74) | copy-start | bytes 786436
  464.9 55.1 %copy-start.64 = (f32[2,128]{1,0:T(2,128)S(1)}, f32[2,128]{1,0:T(2,128)}, u32[]{:S(2)}) copy-start(f32[2,128]{1,0:T(2,128)} %copy-done.62) | copy-start | bytes 3076
  464.9 61.2 %copy-start.61 = (f32[1024]{0:T(1024)S(1)}, f32[1024]{0:T(1024)}, u32[]{:S(2)}) copy-start(f32[1024]{0:T(1024)} %copy-done.60) | copy-start | bytes 12292
  464.9 61.2 %copy-start.66 = (f32[1024]{0:T(1024)S(1)}, f32[1024]{0:T(1024)}, u32[]{:S(2)}) copy-start(f32[1024]{0:T(1024)} %copy-done.65) | copy-start | bytes 12292
  464.9 61.2 %copy-start.68 = (f32[1024,1]{0,1:T(1,128)S(1)}, f32[1024,1]{0,1:T(1,128)}, u32[]{:S(2)}) copy-start(f32[1024,1]{0,1:T(1,128)} %get-tuple-element.295) | copy-start | bytes 12292
  464.9 61.2 %copy-start.71 = (f32[1024,1]{0,1:T(1,128)S(1)}, f32[1024,1]{0,1:T(1,128)}, u32[]{:S(2)}) copy-start(f32[1024,1]{0,1:T(1,128)} %get-tuple-element.297) | copy-start | bytes 12292
  479.9 46.2 %copy-start.25 = (bf16[1024,640]{1,0:T(8,128)(2,1)S(1)}, bf16[1024,640]{1,0:T(8,128)(2,1)}, u32[]{:S(2)}) copy-start(bf16[1024,640]{1,0:T(8,128)(2,1)} %all-gather.15.cloned.1.call-done) | copy-start | bytes 3932164
  539.3 274.6 %reduce-scatter.11.cloned.1.call-start = ((), (), s32[]{:S(2)}) async-start(), calls=%async_computation.13 | async-start | bytes 2162688 | tf_op jit(solution)/shard_map/reduce_scatter | solution.py:245
  539.4 14.8 %copy-start.51 = (bf16[4096,128]{1,0:T(8,128)(2,1)S(1)}, bf16[4096,128]{1,0:T(8,128)(2,1)}, u32[]{:S(2)}) copy-start(bf16[4096,128]{1,0:T(8,128)(2,1)} %all-gather.25.cloned.1.call-done) | copy-start | bytes 3145732
  621.0 331.2 %reduce-scatter.15.cloned.1.call-start = ((), (), s32[]{:S(2)}) async-start(), calls=%async_computation.15 | async-start | bytes 2703360
  758.8 331.6 %reduce-scatter.13.cloned.1.call-start = ((), (), s32[]{:S(2)}) async-start(), calls=%async_computation.14 | async-start | bytes 2703360
  (70 other events, 316.7 us)
Sparse Core Ops, SparseCore 0:
  10.8 56.9 all-gather.12
  70.7 68.0 all-gather.10
  141.7 52.7 all-gather.14
  197.2 55.0 all-gather.16
  255.0 75.8 all-gather.18
  333.7 52.2 all-gather.20
  388.8 76.0 all-gather.22
  467.7 52.2 all-gather.24
  539.5 137.4 reduce-scatter.8
  679.6 134.2 reduce-scatter.10
  816.8 135.3 reduce-scatter.14
  954.9 135.4 reduce-scatter.12
where the time goes:
time: 1110 us; the launch traced here: 1100 us
  waiting for transfers between devices  535 us (48%)
  matrix products  325 us (29%)
  local copies, waits for them, and re-layouts  83.9 us (8%)
  blocking collectives  80.3 us (7%)
  other arithmetic  55.7 us (5%)
  between operations  15.6 us (1%)
    unnamed x14, waiting for transfers between devices  282 us
    dot_general x14, matrix products, against(): lax.dot_general(left, right, (((1,), (1,)), ((), ())), preferred_element_...  124 us
    dot_general x14, matrix products, product(): return jnp.dot(left, right, preferred_element_type=jnp.float32)  66.4 us
    all_gather x1, blocking collectives, local(): lax.all_gather(norm_gain, ('dp', 'fsdp'), axis=0, tiled=True)  43.5 us
    all_gather x1, waiting for transfers between devices, local(): lax.all_gather(widen_out, ('dp', 'fsdp'), axis=0, tiled=True)  43.3 us
    dot_general x4, matrix products, scores_of(): jnp.einsum('qhd,khd->hqk', query_one, key_one, preferred_element_type=jnp...  41.1 us
    all_gather x1, waiting for transfers between devices, local(): lax.all_gather(ff_widen, ('dp', 'fsdp'), axis=0, tiled=True)  40.5 us
    all_gather x1, waiting for transfers between devices, local(): lax.all_gather(ff_narrow, ('dp', 'fsdp'), axis=0, tiled=True)  40.1 us
  transfers between devices with their start and end apart: 12, of which 9 were waited for; matrix products, arithmetic and copies ran while one was open for 40% of the time, Pallas kernels for 0%

commit v1 on v0

v1 whole, which is shorter than its diff:
```python
import functools, math
import jax
import jax.numpy as jnp
from jax import lax
from jax.experimental import pallas as pl
from jax.experimental.pallas import tpu as pltpu
from jax.sharding import PartitionSpec as P

MESH = pl.DeviceIdType.MESH


class Grid:
    def __init__(self, sizes):
        self.dp, self.fsdp = sizes["dp"], sizes["fsdp"]
        if (self.dp, self.fsdp) == (8, 4):
            self.dims = {"z": ("dp", 2, 4), "y": ("dp", 1, 2), "x": ("fsdp", 2, 2), "c": ("fsdp", 1, 2)}
        elif (self.dp, self.fsdp) == (64, 4):
            self.dims = {"z": ("dp", 8, 8), "y": ("dp", 2, 4), "x": ("fsdp", 1, 4), "c": ("dp", 1, 2)}
        else:
            self.dims = {"z": ("dp", 1, self.dp), "y": ("dp", 1, 1), "x": ("fsdp", self.fsdp, 1), "c": ("fsdp", 1, self.fsdp)}
        self.n = {k: v[2] for k, v in self.dims.items()}
        self.devices = self.dp * self.fsdp
        self.planes = self.devices // self.n["z"]

    def stride(self, k):
        axis, step, _ = self.dims[k]
        return step * (self.fsdp if axis == "dp" else 1)

    def here(self):
        idx = {"dp": lax.axis_index("dp"), "fsdp": lax.axis_index("fsdp")}
        return {k: (idx[axis] // step) % size for k, (axis, step, size) in self.dims.items()}

    def device(self, pos):
        out = {"dp": 0, "fsdp": 0}
        for k, (axis, step, _) in self.dims.items():
            out[axis] = out[axis] + pos[k] * step
        return out["dp"], out["fsdp"]

    def slot(self, y, x, c):
        return y * self.stride("y") + x * self.stride("x") + c * self.stride("c")


def barrier_with(grid, here):
    barrier = pltpu.get_barrier_semaphore()
    count = 0
    for k in ("z", "y", "x", "c"):
        n = grid.n[k]
        for step in range(1, n):
            to = (here[k] + step) % n
            pl.semaphore_signal(barrier, inc=1, device_id=grid.device({**here, k: to}), device_id_type=MESH)
            count += 1
    pl.semaphore_wait(barrier, count)


class Gather:
    @staticmethod
    def parts(grid):
        return grid.n["z"] if grid.n["z"] <= 4 else 1

    @staticmethod
    def sem_total(grid):
        z, a, b, c = (grid.n[k] for k in ("z", "y", "x", "c"))
        k = Gather.parts(grid)
        return z + k * a + k * a * b + a * b

    def __init__(self, grid, here, src, out, send, recv, local):
        self.g, self.here, self.src, self.out = grid, here, src, out
        self.send, self.recv, self.local = send, recv, local
        self.k = Gather.parts(grid)
        self.nz, self.n2, self.n3 = grid.n["z"], grid.n["y"], grid.n["x"]
        self.base2 = self.nz
        self.base3 = self.base2 + self.k * self.n2
        self.base4 = self.base3 + self.k * self.n2 * self.n3
        self.sends = []
        self.first = here["c"] == 0
        self.p2 = jnp.where(self.first, here["y"], here["x"])
        self.p3 = jnp.where(self.first, here["x"], here["y"])

    def dev(self, z=None, p2=None, p3=None, c=None):
        h = self.here
        p2 = self.p2 if p2 is None else p2
        p3 = self.p3 if p3 is None else p3
        return self.g.device({
            "z": h["z"] if z is None else z,
            "y": jnp.where(self.first, p2, p3),
            "x": jnp.where(self.first, p3, p2),
            "c": h["c"] if c is None else c,
        })

    def m(self, p2, p3):
        return self.g.slot(jnp.where(self.first, p2, p3), jnp.where(self.first, p3, p2), self.here["c"])

    def part(self, i):
        return (self.here["z"] ^ i) if self.k == self.nz and self.nz & (self.nz - 1) == 0 else None

    def block(self, z, p2, p3):
        return self.out.at[:, self.m(p2, p3)] if z is None else self.out.at[z, self.m(p2, p3)]

    def push(self, src, dst, sem, dev):
        copy = pltpu.make_async_remote_copy(src_ref=src, dst_ref=dst, send_sem=self.send.at[sem], recv_sem=self.recv.at[sem], device_id=dev, device_id_type=MESH)
        copy.start()
        self.sends.append(copy)

    def pull(self, dst, sem):
        pltpu.make_async_remote_copy(src_ref=dst, dst_ref=dst, send_sem=self.send.at[sem], recv_sem=self.recv.at[sem], device_id=self.dev(), device_id_type=MESH).wait_recv()

    def sem2(self, z, p2):
        return self.base2 + (0 if z is None else z * self.n2) + p2

    def sem3(self, z, p2, p3):
        return self.base3 + ((0 if z is None else z * self.n2) + p2) * self.n3 + p3

    def send2(self, z, src=None):
        ref = self.block(z, self.p2, self.p3)
        for d in range(1, self.n2):
            self.push(ref if src is None else src, ref, self.sem2(z, self.p2), self.dev(p2=(self.p2 + d) % self.n2))

    def send3(self, z, p2, src=None):
        ref = self.block(z, p2, self.p3)
        for d in range(1, self.n3):
            self.push(ref if src is None else src, ref, self.sem3(z, p2, self.p3), self.dev(p3=(self.p3 + d) % self.n3))

    def core(self, p2, p3):
        if self.g.n["c"] > 1:
            ref = self.block(None, p2, p3)
            y, x = jnp.where(self.first, p2, p3), jnp.where(self.first, p3, p2)
            self.push(ref, ref, self.base4 + y * self.n3 + x, self.dev(c=1 - self.here["c"]))

    def begin(self):
        z = self.here["z"]
        m0 = self.m(self.p2, self.p3)
        self.own = pltpu.make_async_copy(self.src, self.out.at[z, m0], self.local)
        self.own.start()
        for i in range(1, self.nz):
            to = self.here["z"] ^ i if self.nz & (self.nz - 1) == 0 else (z + i) % self.nz
            self.push(self.src, self.out.at[z, m0], z, self.dev(z=to))
        if self.part(0) is not None:
            self.send3(z, self.p2, self.src)
            self.send2(z, self.src)

    def z_step(self, i):
        z = self.here["z"] ^ i if self.nz & (self.nz - 1) == 0 else (self.here["z"] + i) % self.nz
        self.pull(self.out.at[z, self.m(self.p2, self.p3)], z)
        if self.part(i) is not None:
            self.send2(z)
            self.send3(z, self.p2)

    def z_end(self):
        self.own.wait()
        if self.part(0) is None:
            self.send2(None)
            self.send3(None, self.p2)
        self.core(self.p2, self.p3)

    def step2(self, i):
        z = self.part(i)
        for d in range(1, self.n2):
            q = (self.p2 + d) % self.n2
            self.pull(self.block(z, q, self.p3), self.sem2(z, q))
            self.send3(z, q)

    def end2(self):
        for d in range(1, self.n2):
            self.core((self.p2 + d) % self.n2, self.p3)

    def step3(self, j):
        p2 = (self.p2 + j) % self.n2
        for d in range(1, self.n3):
            q = (self.p3 + d) % self.n3
            for i in range(self.k):
                z = self.part(i)
                self.pull(self.block(z, p2, q), self.sem3(z, p2, q))
            self.core(p2, q)

    def end(self):
        if self.g.n["c"] > 1:
            for y in range(self.n2):
                for x in range(self.n3):
                    self.pull(self.out.at[:, self.g.slot(y, x, 1 - self.here["c"])], self.base4 + y * self.n3 + x)

    def steps(self):
        out = [self.begin]
        out += [functools.partial(self.z_step, i) for i in range(1, self.nz)] + [self.z_end]
        out += [functools.partial(self.step2, i) for i in range(self.k)] + [self.end2]
        out += [functools.partial(self.step3, j) for j in range(self.n2)]
        return out

    def finish(self):
        self.end()
        for copy in self.sends:
            copy.wait_send()


def run_skewed(all_steps, lag):
    count = max(len(s) for s in all_steps)
    for slot in range(count + lag * (len(all_steps) - 1)):
        for i, steps in enumerate(all_steps):
            k = slot - lag * i
            if 0 <= k < len(steps):
                steps[k]()

SETS = 8
R = 16


def normalize(values, gain, shift):
    center = values - jnp.mean(values, axis=-1, keepdims=True)
    spread = jnp.mean(center * center, axis=-1, keepdims=True)
    return center * lax.rsqrt(spread + 1e-12) * gain + shift


def against(left, right):
    return lax.dot_general(
        left, right, (((1,), (1,)), ((), ())), preferred_element_type=jnp.float32
    )


def over_rows(left, right):
    return lax.dot_general(
        left, right, (((0,), (0,)), ((), ())), preferred_element_type=jnp.float32
    )


def product(left, right):
    return jnp.dot(left, right, preferred_element_type=jnp.float32)


def gelu_exact(values):
    return jax.nn.gelu(values, approximate=False)


def gather_kernel(grid, count, lag, first, *refs):
    srcs, outs = refs[:count], refs[count:2*count]
    send, recv, local = refs[2*count:]
    here = grid.here()
    barrier_with(grid, here)
    gs = [Gather(grid, here, srcs[i], outs[i], send.at[i], recv.at[i], local.at[i]) for i in range(count)]
    steps = [g.steps() for g in gs]
    if first:
        for s in steps:
            s.pop(0)()
    run_skewed(steps, lag)
    for g in gs:
        g.finish()

def all_gather(grid, arrays, cid=0, lag=1, first=True):
    count = len(arrays)
    total = Gather.sem_total(grid)
    out_shape = [jax.ShapeDtypeStruct((grid.n["z"], grid.planes) + a.shape, a.dtype) for a in arrays]
    return pl.pallas_call(
        functools.partial(gather_kernel, grid, count, lag, first),
        out_shape=out_shape,
        in_specs=[pl.BlockSpec(memory_space=pltpu.VMEM)] * count,
        out_specs=[pl.BlockSpec(memory_space=pl.ANY)] * count,
        scratch_shapes=[pltpu.SemaphoreType.DMA((count, total)), pltpu.SemaphoreType.DMA((count, total)), pltpu.SemaphoreType.DMA((count,))],
        compiler_params=pltpu.CompilerParams(collective_id=cid, has_side_effects=True, vmem_limit_bytes=8*2**20),
        name="gather",
    )(*arrays)


class Scatter:
    @staticmethod
    def sem_total(grid):
        return 1 + grid.n["x"] + grid.n["y"] + grid.n["z"]

    @staticmethod
    def scratch(grid, shape, dtype=jnp.bfloat16):
        rows, cols = shape
        z, y, x = grid.n["z"], grid.n["y"], grid.n["x"]
        out = []
        if grid.n["c"] > 1:
            out += [pltpu.VMEM((y * x, z, rows, cols), dtype)] * 2
        out += [pltpu.VMEM((x, y, z, rows, cols), dtype)] * 2
        out += [pltpu.VMEM((y, z, rows, cols), dtype)] * 2
        out += [pltpu.VMEM((z, rows, cols), dtype)] * 2
        out += [pltpu.VMEM((y * x, z, rows, cols), jnp.float32)]
        return out

    def __init__(self, grid, here, src, put, bufs, send, recv):
        self.g, self.here, self.src, self.put, self.send, self.recv = grid, here, src, put, send, recv
        bufs = list(bufs)
        self.two = grid.n["c"] > 1
        self.s1, self.r1 = (bufs.pop(0), bufs.pop(0)) if self.two else (None, None)
        self.s2, self.r2, self.s3, self.r3, self.s4, self.r4, self.acc = bufs
        self.nz, self.n2, self.n3 = grid.n["z"], grid.n["y"], grid.n["x"]
        self.first = here["c"] == 0
        self.p2 = jnp.where(self.first, here["y"], here["x"])
        self.p3 = jnp.where(self.first, here["x"], here["y"])
        self.sends, self.pulls = [], []

    def dev(self, z=None, p2=None, p3=None, c=None):
        h = self.here
        p2 = self.p2 if p2 is None else p2
        p3 = self.p3 if p3 is None else p3
        return self.g.device({
            "z": h["z"] if z is None else z,
            "y": jnp.where(self.first, p2, p3),
            "x": jnp.where(self.first, p3, p2),
            "c": h["c"] if c is None else c,
        })

    def flat(self, p2, p3):
        return jnp.where(self.first, p2 * self.n3 + p3, p3 * self.n3 + p2)

    def push(self, src, dst, sem_s, sem_r, dev):
        copy = pltpu.make_async_remote_copy(src_ref=src, dst_ref=dst, send_sem=self.send.at[sem_s], recv_sem=self.recv.at[sem_r], device_id=dev, device_id_type=MESH)
        copy.start()
        self.sends.append(copy)

    def pull(self, dst, sem):
        pltpu.make_async_remote_copy(src_ref=dst, dst_ref=dst, send_sem=self.send.at[sem], recv_sem=self.recv.at[sem], device_id=self.dev(), device_id_type=MESH).wait_recv()

    def begin(self):
        c = self.here["c"]
        for y in range(self.n2):
            for x in range(self.n3):
                i = y * self.n3 + x
                if self.two:
                    self.s1[i] = self.src[:, self.g.slot(y, x, 1 - c)].astype(self.s1.dtype)
        if self.two:
            self.push(self.s1, self.r1, 0, 0, self.dev(c=1 - c))

    def step1(self):
        c = self.here["c"]
        if self.two:
            self.pull(self.r1, 0)
        for y in range(self.n2):
            for x in range(self.n3):
                i = y * self.n3 + x
                part = self.src[:, self.g.slot(y, x, c)]
                self.acc[i] = part + self.r1[i].astype(jnp.float32) if self.two else part
        for d in range(1, self.n3):
            q = (self.p3 + d) % self.n3
            for j in range(self.n2):
                self.s2[d, j] = self.acc[self.flat(j, q)].astype(self.s2.dtype)
            self.push(self.s2.at[d], self.r2.at[d], 1 + d, 1 + d, self.dev(p3=q))

    def step2(self):
        for d in range(1, self.n3):
            self.pull(self.r2.at[d], 1 + d)
        for j in range(self.n2):
            i = self.flat(j, self.p3)
            total = self.acc[i]
            for d in range(1, self.n3):
                total = total + self.r2[d, j].astype(jnp.float32)
            self.acc[i] = total
        base = 1 + self.n3
        for d in range(1, self.n2):
            q = (self.p2 + d) % self.n2
            self.s3[d] = self.acc[self.flat(q, self.p3)].astype(self.s3.dtype)
            self.push(self.s3.at[d], self.r3.at[d], base + d, base + d, self.dev(p2=q))

    def step3(self):
        base = 1 + self.n3
        i = self.flat(self.p2, self.p3)
        total = self.acc[i]
        for d in range(1, self.n2):
            self.pull(self.r3.at[d], base + d)
            total = total + self.r3[d].astype(jnp.float32)
        self.acc[i] = total
        base = base + self.n2
        self.s4[...] = total.astype(self.s4.dtype)
        z = self.here["z"]
        for d in range(1, self.nz):
            q = (z + d) % self.nz
            self.push(self.s4.at[q], self.r4.at[d], base + d, base + d, self.dev(z=q))

    def step4(self):
        base = 1 + self.n3 + self.n2
        total = self.acc[self.flat(self.p2, self.p3), self.here["z"]]
        for d in range(1, self.nz):
            self.pull(self.r4.at[d], base + d)
            total = total + self.r4[d].astype(jnp.float32)
        self.put(total)

    def steps(self):
        return [self.begin, self.step1, self.step2, self.step3, self.step4]

    def finish(self):
        for copy in self.sends:
            copy.wait_send()


def scatter_kernel(grid, places, nout, *refs):
    count = len(places)
    srcs, outs = refs[:count], refs[count:count + nout]
    rest = refs[count + nout:]
    send, recv = rest[:2]
    rest = rest[2:]
    per = len(rest) // count
    here = grid.here()
    barrier_with(grid, here)
    units = []
    for i, (o, col) in enumerate(places):
        def put(total, o=o, col=col):
            outs[o][:, col:col + total.shape[1]] = total
        units.append(Scatter(grid, here, srcs[i], put, rest[i * per:(i + 1) * per], send.at[i], recv.at[i]))
    run_skewed([u.steps() for u in units], 1)
    for u in units:
        u.finish()


def reduce_scatter(grid, arrays, places, outs, cid):
    count = len(arrays)
    views = [a.reshape(grid.n["z"], grid.planes, a.shape[0] // grid.devices, a.shape[1]) for a in arrays]
    total = Scatter.sem_total(grid)
    scratch = [pltpu.SemaphoreType.DMA((count, total)), pltpu.SemaphoreType.DMA((count, total))]
    for v in views:
        scratch += Scatter.scratch(grid, v.shape[2:])
    return pl.pallas_call(
        functools.partial(scatter_kernel, grid, places, len(outs)),
        out_shape=[jax.ShapeDtypeStruct(o, jnp.float32) for o in outs],
        in_specs=[pl.BlockSpec(memory_space=pltpu.VMEM)] * count,
        out_specs=[pl.BlockSpec(memory_space=pltpu.VMEM)] * len(outs),
        scratch_shapes=scratch,
        compiler_params=pltpu.CompilerParams(collective_id=cid, has_side_effects=True, vmem_limit_bytes=60 * 2**20),
        name="scatter",
    )(*views)

HD=64
def dotf(a,b,ca,cb):
    return lax.dot_general(a,b,(((ca,),(cb,)),((),())),preferred_element_type=jnp.float32)

def set_bias(bias, row, col, half):
    n=bias.shape[0]
    i=lax.broadcasted_iota(jnp.int32,(n,n),0); j=lax.broadcasted_iota(jnp.int32,(n,n),1)
    near=jnp.abs(i-j)<=half
    ok=near|(jnp.broadcast_to(row,(n,n))>0)|(jnp.broadcast_to(col,(n,n))>0)
    bias[...]=jnp.where(ok,0.0,-1e30)

def fwd_kernel(half,row_ref,col_ref,q_ref,k_ref,v_ref,o_ref,p_ref,bias):
    @pl.when(pl.program_id(1)==0)
    def _(): set_bias(bias,row_ref[0],col_ref[0],half)
    width=q_ref.shape[1]
    q=q_ref[...]; k=k_ref[...]
    vt=v_ref[...].T
    outs=[]
    for h in range(width//HD):
        c=(h*HD)//128*128
        lane=lax.broadcasted_iota(jnp.int32,(1,128),1)//HD
        keep=(lane==(h*HD-c)//HD)
        kh=jnp.where(keep,k[:,c:c+128],jnp.zeros((),k.dtype))*jnp.asarray(HD**-0.5,k.dtype)
        s=dotf(kh,q[:,c:c+128],1,1)+bias[...]
        top=jnp.max(s,axis=0,keepdims=True)
        e=jnp.exp(s-top)
        tot=jnp.sum(e,axis=0,keepdims=True)
        p=(e*(1.0/tot)).astype(jnp.bfloat16)
        p_ref[h]=p
        outs.append(dotf(vt[h*HD:(h+1)*HD],p,1,0))
    o_ref[...]=jnp.concatenate(outs,axis=0).T.astype(o_ref.dtype)

def attn_fwd(q,k,v,row,col,seqs,length,per=2):
    rows,width=q.shape; heads=width//HD
    w=per*HD
    spec=pl.BlockSpec((length,w),lambda s,h:(s,h))
    return pl.pallas_call(functools.partial(fwd_kernel,256),grid=(seqs,heads//per),
      in_specs=[pl.BlockSpec((1,1,length),lambda s,h:(s,0,0)),pl.BlockSpec((1,length,1),lambda s,h:(s,0,0)),spec,spec,spec],
      out_specs=[spec,pl.BlockSpec((None,per,length,length),lambda s,h:(s,h,0,0))],
      out_shape=[jax.ShapeDtypeStruct(q.shape,q.dtype),jax.ShapeDtypeStruct((seqs,heads,length,length),q.dtype)],
      scratch_shapes=[pltpu.VMEM((length,length),jnp.float32)],
      compiler_params=pltpu.CompilerParams(vmem_limit_bytes=48*2**20),name="attend")(row,col,q,k,v)

def bwd_kernel(q_ref,k_ref,v_ref,p_ref,d_ref,dq_ref,dk_ref,dv_ref):
    width=q_ref.shape[1]
    q=q_ref[...]; k=k_ref[...]; v=v_ref[...]; d=d_ref[...]
    scale=jnp.asarray(HD**-0.5,q.dtype)
    kt=(k*scale).T
    qs=q*scale
    dqs=[]; dks=[]; dvs=[]
    lane=lax.broadcasted_iota(jnp.int32,(1,128),1)//HD
    for h in range(width//HD):
        c=(h*HD)//128*128
        keep=(lane==(h*HD-c)//HD)
        vh=jnp.where(keep,v[:,c:c+128],jnp.zeros((),v.dtype))
        pb=p_ref[h]
        p=pb.astype(jnp.float32)
        dp=dotf(vh,d[:,c:c+128],1,1)
        t=p*dp
        inner=jnp.sum(t,axis=0,keepdims=True)
        ds=(t-p*inner).astype(jnp.bfloat16)
        dqs.append(dotf(kt[h*HD:(h+1)*HD],ds,1,0))
        dks.append(dotf(ds,qs[:,c:c+128],1,0))
        dvs.append(dotf(pb,d[:,c:c+128],1,0))
    dq_ref[...]=jnp.concatenate(dqs,axis=0).T.astype(dq_ref.dtype)
    for g in range(width//128):
        keep=lane==0
        dk_ref[:,g*128:(g+1)*128]=jnp.where(keep,dks[2*g],dks[2*g+1]).astype(dk_ref.dtype)
        dv_ref[:,g*128:(g+1)*128]=jnp.where(keep,dvs[2*g],dvs[2*g+1]).astype(dv_ref.dtype)

def attn_bwd(q,k,v,p,d,seqs,length,per=2):
    rows,width=q.shape; heads=width//HD; w=per*HD
    spec=pl.BlockSpec((length,w),lambda s,h:(s,h))
    return pl.pallas_call(bwd_kernel,grid=(seqs,heads//per),
      in_specs=[spec,spec,spec,pl.BlockSpec((None,per,length,length),lambda s,h:(s,h,0,0)),spec],
      out_specs=[spec]*3,out_shape=[jax.ShapeDtypeStruct(q.shape,q.dtype)]*3,
      compiler_params=pltpu.CompilerParams(vmem_limit_bytes=48*2**20),name="attend_back")(q,k,v,p,d)


def local(sizes, tokens, cotangent, adapter_id, global_pos, w_qkv, w_out, w_up, w_down, norm_gain, norm_bias,
          narrow_in, widen_out, ff_narrow, ff_widen):
    grid = Grid(sizes)
    small = jnp.concatenate([norm_gain, norm_bias], axis=1).T
    share = small.shape[1]
    small = jnp.pad(small, ((0, 12), (0, 128 - share)))
    got = all_gather(grid, [w_qkv, narrow_in, widen_out, small, w_out, w_up, w_down, ff_narrow, ff_widen], 0, 2, True)

    def whole(a):
        return a.reshape(-1, a.shape[-1])

    wq_full, a_full, b_full, small_full, wo_full, wu_full, wd_full, ffa_full, ffb_full = [whole(a) for a in got]
    norms = small_full.reshape(grid.devices, 16, 128)[:, :4, :share].transpose(1, 0, 2).reshape(4, grid.devices * share)
    norms = norms.astype(jnp.float32)
    gain_one, gain_two, shift_one, shift_two = norms[0], norms[1], norms[2], norms[3]
    seq_local, length, model_width = tokens.shape
    rows_all = seq_local * length
    set_cols = SETS * R
    chosen = (
        lax.broadcasted_iota(jnp.int32, (seq_local, set_cols), 1) // R == adapter_id[:, None]
    ).astype(jnp.float32)
    chosen = jnp.broadcast_to(chosen[:, None, :], (seq_local, length, set_cols)).reshape(rows_all, set_cols)
    chosen_three = jnp.concatenate([chosen, chosen, chosen], axis=1)
    positions = lax.broadcasted_iota(jnp.int32, (length,), 0)
    is_global = jnp.any(global_pos[:, :, None] == positions[None, None, :], axis=1).astype(jnp.float32)

    def cols_of(slot):
        return slice(slot * set_cols, (slot + 1) * set_cols)

    flat_in = tokens.reshape(rows_all, model_width)
    t_qkv = (product(flat_in, a_full[:, : 3 * set_cols]) * chosen_three).astype(jnp.bfloat16)
    projected = []
    for slot in range(3):
        summed = product(flat_in, wq_full[:, slot * model_width : (slot + 1) * model_width]) + against(
            t_qkv[:, cols_of(slot)], b_full[:, cols_of(slot)]
        )
        projected.append(summed.astype(jnp.bfloat16))
    query_low, key_low, value_low = projected
    mixed_flat, weights_low = attn_fwd(query_low, key_low, value_low, is_global[:, None, :], is_global[:, :, None], seq_local, length, 4)
    t_out = (product(mixed_flat, a_full[:, cols_of(3)]) * chosen).astype(jnp.bfloat16)
    attn_out = product(mixed_flat, wo_full) + against(t_out, b_full[:, cols_of(3)])
    resid = flat_in.astype(jnp.float32) + attn_out
    normed, norm_one_back = jax.vjp(lambda values: normalize(values, gain_one, shift_one), resid)
    normed_low = normed.astype(jnp.bfloat16)
    t_up = (product(normed_low, a_full[:, cols_of(4)]) * chosen).astype(jnp.bfloat16)
    pre_act = product(normed_low, wu_full) + against(t_up, ffb_full)
    cdf = 0.5 * (1.0 + lax.erf(pre_act * (0.5 ** 0.5)))
    act_low = (pre_act * cdf).astype(jnp.bfloat16)
    slope = cdf + pre_act * jnp.exp(-0.5 * pre_act * pre_act) * ((0.5 / math.pi) ** 0.5)
    act_low, slope = lax.optimization_barrier((act_low, slope))
    t_down = (product(act_low, ffa_full) * chosen).astype(jnp.bfloat16)
    down_out = product(act_low, wd_full) + against(t_down, b_full[:, cols_of(4)])
    final = normed + down_out
    result, norm_two_back = jax.vjp(lambda values: normalize(values, gain_two, shift_two), final)
    d_final = norm_two_back(cotangent.reshape(rows_all, model_width).astype(jnp.float32))[0]
    d_down = d_final.astype(jnp.bfloat16)
    dt_down = (product(d_down, b_full[:, cols_of(4)]) * chosen).astype(jnp.bfloat16)
    grad_b_down = over_rows(d_down, t_down)
    grad_ff_narrow = over_rows(act_low, dt_down)
    d_act = against(d_down, wd_full) + against(dt_down, ffa_full)
    d_pre = (d_act * slope).astype(jnp.bfloat16)
    dt_up = (product(d_pre, ffb_full) * chosen).astype(jnp.bfloat16)
    grad_ff_widen = over_rows(d_pre, t_up)
    grad_a_up = over_rows(normed_low, dt_up)
    d_normed = d_final + against(d_pre, wu_full) + against(dt_up, a_full[:, cols_of(4)])
    d_resid = norm_one_back(d_normed)[0]
    d_attn = d_resid.astype(jnp.bfloat16)
    dt_out = (product(d_attn, b_full[:, cols_of(3)]) * chosen).astype(jnp.bfloat16)
    grad_b_out = over_rows(d_attn, t_out)
    grad_a_out = over_rows(mixed_flat, dt_out)
    d_mixed = (against(d_attn, wo_full) + against(dt_out, a_full[:, cols_of(3)])).astype(jnp.bfloat16)
    d_parts = attn_bwd(query_low, key_low, value_low, weights_low, d_mixed, seq_local, length, 4)
    dt_parts = [
        (product(d_parts[slot], b_full[:, cols_of(slot)]) * chosen).astype(jnp.bfloat16) for slot in range(3)
    ]
    dt_qkv = jnp.concatenate(dt_parts, axis=1)
    grad_b_qkv = [over_rows(d_parts[slot], t_qkv[:, cols_of(slot)]) for slot in range(3)]
    grad_a_qkv = over_rows(flat_in, dt_qkv)
    d_input = d_resid + against(dt_qkv, a_full[:, : 3 * set_cols])
    for slot in range(3):
        d_input = d_input + against(d_parts[slot], wq_full[:, slot * model_width : (slot + 1) * model_width])
    rows_own, ff_own = model_width // grid.devices, ff_narrow.shape[0]
    late = reduce_scatter(
        grid, [grad_ff_narrow, grad_ff_widen, grad_a_out, grad_a_up, grad_b_out, grad_b_down],
        [(0, 0), (1, 0), (2, 0), (2, set_cols), (3, 0), (3, set_cols)],
        [(ff_own, set_cols), (ff_own, set_cols), (rows_own, 2 * set_cols), (rows_own, 2 * set_cols)], 1)
    early = reduce_scatter(
        grid, [grad_a_qkv] + grad_b_qkv, [(0, 0), (1, 0), (1, set_cols), (1, 2 * set_cols)],
        [(rows_own, 3 * set_cols), (rows_own, 3 * set_cols)], 2)
    return (
        result.reshape(seq_local, length, model_width).astype(jnp.bfloat16),
        d_input.reshape(seq_local, length, model_width).astype(jnp.bfloat16),
        jnp.concatenate([early[0], late[2]], axis=1),
        jnp.concatenate([early[1], late[3]], axis=1),
        late[0],
        late[1],
    )


def solution(mesh):
    rows = P(("dp", "fsdp"), None)
    cube = P(("dp", "fsdp"), None, None)
    in_specs = (cube, cube, P(("dp", "fsdp"))) + (rows,) * 11
    out_specs = (cube, cube) + (rows,) * 4
    return jax.shard_map(functools.partial(local, dict(mesh.shape)), mesh=mesh, in_specs=in_specs, out_specs=out_specs, check_vma=False)
```

time: 1110 us -> 482 us (0.43)
  waiting for transfers between devices: 535 us -> 0 us
  Pallas kernels: 0 us -> 263 us
  matrix products: 325 us -> 162 us
  blocking collectives: 80.3 us -> 0 us
  local copies, waits for them, and re-layouts: 83.9 us -> 32.3 us
  other arithmetic: 55.7 us -> 13.6 us
  between operations: 15.6 us -> 1.73 us
    unnamed x14 -> x0, waiting for transfers between devices: 282 us -> none
    pallas_call x0 -> x5, Pallas kernels: none -> 263 us  [the longest x1 134 us: all_gather(): pl.pallas_call(functools.partial(gather_kernel, grid, count, lag, first),...]
    all_gather x8 -> x0, waiting for transfers between devices: 225 us -> none  [the longest x1 43.3 us: local(): lax.all_gather(widen_out, ('dp', 'fsdp'), axis=0, tiled=True)]
    dot_general x14 -> x0, matrix products: 116 us -> none  [the longest x4 41.1 us: scores_of(): jnp.einsum('qhd,khd->hqk', query_one, key_one, preferred_element_type=jnp...]
    all_gather x2 -> x0, blocking collectives: 80.3 us -> none  [the longest x1 43.5 us: local(): lax.all_gather(norm_gain, ('dp', 'fsdp'), axis=0, tiled=True)]
    dot_general x14 -> x16, matrix products: 124 us -> 89.1 us  [against(): lax.dot_general(left, right, (((1,), (1,)), ((), ())), preferred_element_...]
    reduce_scatter x2 -> x0, waiting for transfers between devices: 29 us -> none  [the longest x1 29 us: local(): lax.psum_scatter(grad_ff_widen, ('dp', 'fsdp'), scatter_dimension=0, tile...]
    dynamic_update_slice x14 -> x0, local copies, waits for them, and re-layouts: 25.2 us -> none  [local(): lax.map(attend, (query_heads, key_heads, value_heads, is_global))]
  transfers between devices with their start and end apart: 12 -> 0, of which waited for: 9 -> 0; matrix products, arithmetic and copies ran while one was open for 40% -> 0% of each run, Pallas kernels for 0% -> 0%
where the time goes in v1:
time: 482 us; the launch traced here: 472 us
  Pallas kernels  263 us (55%)
  matrix products  162 us (34%)
  local copies, waits for them, and re-layouts  32.3 us (7%)
  other arithmetic  13.6 us (3%)
    pallas_call x1, Pallas kernels, all_gather(): pl.pallas_call(functools.partial(gather_kernel, grid, count, lag, first),...  134 us
    dot_general x16, matrix products, against(): lax.dot_general(left, right, (((1,), (1,)), ((), ())), preferred_element_...  89.1 us
    pallas_call x2, Pallas kernels, reduce_scatter(): pl.pallas_call(functools.partial(scatter_kernel, grid, places, len(outs))...  73.3 us
    dot_general x16, matrix products, product(): return jnp.dot(left, right, preferred_element_type=jnp.float32)  52.2 us
    pallas_call x1, Pallas kernels, attn_bwd(): pl.pallas_call(bwd_kernel, grid=(seqs, heads // per), in_specs=[spec, spe...  30 us
    unnamed x131, local copies, waits for them, and re-layouts  28.4 us
    pallas_call x1, Pallas kernels, attn_fwd(): pl.pallas_call(functools.partial(fwd_kernel, 256), grid=(seqs, heads // p...  25.1 us
    dot_general x10, matrix products, over_rows(): lax.dot_general(left, right, (((0,), (0,)), ((), ())), preferred_element_...  20.6 us

profile of v1, /device:TPU:0, one launch (start us, length us, event | category | flops | bytes accessed | tf_op | source)
XLA Modules:
  0.0 472.4 jit_solution(14516244903138274934)
XLA Ops:
  11.0 134.4 %gather.1 = (bf16[4,8,32,3072]{3,2,1,0:T(8,128)(2,1)S(1)}, bf16[4,8,32,640]{3,2,1,0:T(8,128)(2,1)S(1)}, bf16[4,8,32,640]{3,2,1,0:T(8,128)(2,1)S(1)}, bf16[4,8,16...) custom-call(bf16[32,3072]{1,0:T(8,128)(2,1)S(1)} %copy-done.12, ...), custom_call_target="tpu_custom_call" | custom-call | tf_op jit(solution)/shard_map/gather/pallas_call | solution.py:250
  147.5 3.2 copy-done.18
  150.8 3.3 copy-done.19
  158.6 3.4 fusion.20
  163.6 3.7 fusion.7.v_ref
  168.0 3.7 fusion.8.k_ref
  174.8 25.1 %attend.1 = (bf16[1024,1024]{1,0:T(8,128)(2,1)S(1)}, bf16[2,16,512,512]{3,2,1,0:T(8,128)(2,1)}) custom-call(f32[2,1,512]{2,1,0:T(1,128)S(1)} %reshape.221.row_ref, f32[2,512,1]{2,1,0:T(8,128)S(1)} %copy.45.col_ref, bf16[1024,1024]{1,0:T(8,128)(2,1)S(1)} %fusion.9.q_ref, bf16[1024,1024]{1,0:T(8,128)(2,1)} %fusion.8.k_ref, bf16[1024,1024]{1,0:T(8,128)(2,1)} %fusion.7.v_ref), custom_call_target="tpu_custom_call" | custom-call | tf_op jit(solution)/shard_map/attend/pallas_call | solution.py:456
  210.8 11.6 %fusion.69 = f32[1024,4096]{1,0:T(8,128)} fusion(bf16[1024,1024]{1,0:T(8,128)(2,1)S(1)} %fusion.10, bf16[1024,4096]{1,0:T(8,128)(2,1)S(1)} %bitcast.131), kind=kOutput, calls=%fused_computation.128 | convolution fusion | flops 8589934592 | bytes 27262976 | tf_op jit(solution)/shard_map/dot_general | solution.py:225
  222.5 17.9 %fusion.3 = (f32[1024,4096]{1,0:T(8,128)}, bf16[1024,4096]{1,0:T(8,128)(2,1)S(1)}) fusion(f32[1024,4096]{1,0:T(8,128)} %fusion.69, bf16[1024,128]{0,1:T(8,128)(2,1)S(1)} %fusion.24, bf16[4096,128]{1,0:T(8,128)(2,1)S(1)} %bitcast.125), kind=kOutput, calls=%fused_computation.4 | convolution fusion | flops 1119879168 | bytes 43253760 | tf_op jit(solution)/shard_map/dot_general | solution.py:213
  243.3 8.8 %fusion.70 = f32[1024,1024]{1,0:T(8,128)S(1)} fusion(bf16[1024,4096]{1,0:T(8,128)(2,1)S(1)} %get-tuple-element.36, bf16[4096,1024]{1,0:T(8,128)(2,1)S(1)} %bitcast.134), kind=kOutput, calls=%fused_computation.129 | convolution fusion | flops 8589934592 | bytes 20971520 | tf_op jit(solution)/shard_map/dot_general | solution.py:225
  255.0 3.5 fusion.65
  260.6 3.7 fusion.74
  265.9 13.6 %fusion.71 = f32[1024,4096]{1,0:T(8,128)} fusion(bf16[1024,1024]{1,0:T(8,128)(2,1)} %copy-done.37, bf16[4096,1024]{1,0:T(8,128)(2,1)S(1)} %bitcast.135), kind=kOutput, calls=%fused_computation.130 | convolution fusion | flops 8589934592 | bytes 27262976 | tf_op jit(solution)/shard_map/dot_general | solution.py:213
  279.5 15.4 %multiply_convert_fusion = bf16[1024,4096]{1,0:T(8,128)(2,1)} fusion(f32[1024,4096]{1,0:T(8,128)} %get-tuple-element.39, f32[1024,4096]{1,0:T(8,128)} %fusion.71, bf16[1024,128]{0,1:T(8,128)(2,1)} %copy-done.42, bf16[4096,128]{1,0:T(8,128)(2,1)S(1)} %bitcast.118), kind=kOutput, calls=%fused_computation.5 | convolution fusion | flops 1086324736 | bytes 43253760 | tf_op jit(solution)/shard_map/dot_general | solution.py:213
  294.9 13.0 %fusion.72 = f32[1024,1024]{1,0:T(8,128)S(1)} fusion(bf16[1024,4096]{1,0:T(8,128)(2,1)} %multiply_convert_fusion, bf16[1024,4096]{1,0:T(8,128)(2,1)} %bitcast.128), kind=kOutput, calls=%fused_computation.131 | convolution fusion | flops 8589934592 | bytes 20971520 | tf_op jit(solution)/shard_map/dot_general | solution.py:213
  310.8 3.8 fusion.75
  332.9 30.0 %attend_back.1 = (bf16[1024,1024]{1,0:T(8,128)(2,1)S(1)}, bf16[1024,1024]{1,0:T(8,128)(2,1)S(1)}, bf16[1024,1024]{1,0:T(8,128)(2,1)}) custom-call(bf16[1024,1024]{1,0:T(8,128)(2,1)} %copy-done.5, bf16[1024,1024]{1,0:T(8,128)(2,1)} %fusion.8.k_ref, bf16[1024,1024]{1,0:T(8,128)(2,1)} %fusion.7.v_ref, bf16[2,16,512,512]{3,2,1,0:T(8,128)(2,1)} %get-tuple-element.40.p_ref, ...), custom_call_target="tpu_custom_call" | custom-call | tf_op jit(solution)/shard_map/attend_back/pallas_call | solution.py:493
  364.2 43.5 %scatter.3 = (f32[128,128]{1,0:T(8,128)}, f32[128,128]{1,0:T(8,128)}, f32[32,256]{1,0:T(8,128)}, f32[32,256]{1,0:T(8,128)}) custom-call(f32[4,8,128,128]{3,2,1,0:T(8,128)} %bitcast.154, f32[4,8,128,128]{3,2,1,0:T(8,128)} %bitcast.155, f32[4,8,32,128]{3,2,1,0:T(8,128)} %bitcast.159, f32[4,8,32,128]{3,2,1,0:T(8,128)} %bitcast.158, ...), custom_call_target="tpu_custom_call" | custom-call | tf_op jit(solution)/shard_map/scatter/pallas_call | solution.py:410
  418.9 3.1 copy.52
  421.9 29.8 %scatter.2 = (f32[32,384]{1,0:T(8,128)}, f32[32,384]{1,0:T(8,128)}) custom-call(f32[4,8,32,384]{3,2,1,0:T(8,128)} %bitcast.156, f32[4,8,32,128]{3,2,1,0:T(8,128)} %bitcast.161, f32[4,8,32,128]{3,2,1,0:T(8,128)} %bitcast.162, f32[4,8,32,128]{3,2,1,0:T(8,128)} %bitcast.163), custom_call_target="tpu_custom_call" | custom-call | tf_op jit(solution)/shard_map/scatter/pallas_call | solution.py:410
  454.6 4.7 %fusion.11 = f32[1024,1024]{1,0:T(8,128)S(1)} fusion(bf16[1024,1024]{1,0:T(8,128)(2,1)} %get-tuple-element.43, bf16[1024,3072]{1,0:T(8,128)(2,1)} %bitcast.136), kind=kOutput, calls=%fused_computation.34 | convolution fusion | flops 2147483648 | bytes 8388608 | tf_op jit(solution)/shard_map/dot_general | solution.py:213
  459.3 4.0 fusion.14
  463.4 4.1 fusion.17
  467.6 3.4 add_convert_fusion
  (189 shorter events, 80.2 us)
Async XLA Ops:
  158.6 5.0 %copy-start.45 = (bf16[2,512,1024]{2,1,0:T(8,128)(2,1)S(1)}, bf16[2,512,1024]{2,1,0:T(8,128)(2,1)}, u32[]{:S(2)}) copy-start(bf16[2,512,1024]{2,1,0:T(8,128)(2,1)} %param.14) | copy-start | bytes 6291460
  162.0 9.7 %copy-start.40 = (bf16[1024,384]{0,1:T(8,128)(2,1)}, bf16[1024,384]{0,1:T(8,128)(2,1)S(1)}, u32[]{:S(2)}) copy-start(bf16[1024,384]{0,1:T(8,128)(2,1)S(1)} %fusion.20) | copy-start | bytes 2359300
  174.7 27.1 %copy-start.5 = (bf16[1024,1024]{1,0:T(8,128)(2,1)}, bf16[1024,1024]{1,0:T(8,128)(2,1)S(1)}, u32[]{:S(2)}) copy-start(bf16[1024,1024]{1,0:T(8,128)(2,1)S(1)} %fusion.9.q_ref) | copy-start | bytes 6291460
  174.8 25.1 %copy-start.29 = (f32[16,8,2,512]{3,1,2,0:T(8,128)S(1)}, f32[16,8,2,512]{3,1,2,0:T(8,128)}, u32[]{:S(2)}) copy-start(f32[16,8,2,512]{3,1,2,0:T(8,128)} %copy.62) | copy-start | bytes 1572868
  174.8 27.1 %copy-start.23 = (bf16[4,8,32,1024]{3,2,1,0:T(8,128)(2,1)S(1)}, bf16[4,8,32,1024]{3,2,1,0:T(8,128)(2,1)}, u32[]{:S(2)}) copy-start(bf16[4,8,32,1024]{3,2,1,0:T(8,128)(2,1)} %copy-done.22) | copy-start | bytes 6291460
  199.9 4.3 copy-start
  204.2 6.5 %slice-start = ((s8[8388608]{0:T(1024)(128)(4,1)}), s8[4194304]{0:T(1024)(128)(4,1)S(1)}, s32[]{:S(2)}) async-start(s8[8388608]{0:T(1024)(128)(4,1)} %bitcast.129), calls=%async_computation | async-start | bytes 8388608
  205.1 5.6 %slice-start.1 = ((s8[8388608]{0:T(1024)(128)(4,1)}), s8[4194304]{0:T(1024)(128)(4,1)S(1)}, s32[]{:S(2)}) async-start(s8[8388608]{0:T(1024)(128)(4,1)} %bitcast.129), calls=%async_computation.1 | async-start | bytes 8388608
  208.0 14.5 %copy-start.35 = (bf16[1024,1024]{1,0:T(8,128)(2,1)}, bf16[1024,1024]{1,0:T(8,128)(2,1)S(1)}, u32[]{:S(2)}) copy-start(bf16[1024,1024]{1,0:T(8,128)(2,1)S(1)} %fusion.10) | copy-start | bytes 6291460
  208.0 35.3 %slice-start.2 = ((s8[8388608]{0:T(1024)(128)(4,1)}), s8[4194304]{0:T(1024)(128)(4,1)S(1)}, s32[]{:S(2)}) async-start(s8[8388608]{0:T(1024)(128)(4,1)} %bitcast.132), calls=%async_computation.2 | async-start | bytes 8388608
  210.8 11.7 %copy-start.54 = (bf16[1024,128]{0,1:T(8,128)(2,1)}, bf16[1024,128]{0,1:T(8,128)(2,1)S(1)}, u32[]{:S(2)}) copy-start(bf16[1024,128]{0,1:T(8,128)(2,1)S(1)} %fusion.24) | copy-start | bytes 786436
  210.8 11.7 %copy-start.9 = (bf16[4,8,128,128]{3,2,1,0:T(8,128)(2,1)S(1)}, bf16[4,8,128,128]{3,2,1,0:T(8,128)(2,1)}, u32[]{:S(2)}) copy-start(bf16[4,8,128,128]{3,2,1,0:T(8,128)(2,1)} %copy-done.8) | copy-start | bytes 3145732
  210.8 32.4 %slice-start.3 = ((s8[8388608]{0:T(1024)(128)(4,1)}), s8[4194304]{0:T(1024)(128)(4,1)S(1)}, s32[]{:S(2)}) async-start(s8[8388608]{0:T(1024)(128)(4,1)} %bitcast.132), calls=%async_computation.3 | async-start | bytes 8388608
  243.3 8.8 %copy-start.26 = (f32[1024,1024]{1,0:T(8,128)S(1)}, f32[1024,1024]{1,0:T(8,128)}, u32[]{:S(2)}) copy-start(f32[1024,1024]{1,0:T(8,128)} %copy-done.25) | copy-start | bytes 12582916
  258.8 5.6 %copy-start.37 = (bf16[1024,1024]{1,0:T(8,128)(2,1)}, bf16[1024,1024]{1,0:T(8,128)(2,1)S(1)}, u32[]{:S(2)}) copy-start(bf16[1024,1024]{1,0:T(8,128)(2,1)S(1)} %add_convert_fusion.4) | copy-start | bytes 6291460
  294.9 13.0 %copy-start.28 = (bf16[1024,4096]{1,0:T(8,128)(2,1)S(1)}, bf16[1024,4096]{1,0:T(8,128)(2,1)}, u32[]{:S(2)}) copy-start(bf16[1024,4096]{1,0:T(8,128)(2,1)} %multiply_convert_fusion) | copy-start | bytes 25165828
  294.9 13.0 %copy-start.30 = (f32[16,8,2,512]{3,1,2,0:T(8,128)S(1)}, f32[16,8,2,512]{3,1,2,0:T(8,128)}, u32[]{:S(2)}) copy-start(f32[16,8,2,512]{3,1,2,0:T(8,128)} %copy.62) | copy-start | bytes 1572868
  321.5 4.4 copy-start.44
  408.6 8.1 %copy-start.48 = (bf16[1024,128]{0,1:T(8,128)(2,1)}, bf16[1024,128]{0,1:T(8,128)(2,1)S(1)}, u32[]{:S(2)}) copy-start(bf16[1024,128]{0,1:T(8,128)(2,1)S(1)} %fusion.27) | copy-start | bytes 786436
  411.1 5.6 %copy-start.50 = (bf16[1024,128]{0,1:T(8,128)(2,1)}, bf16[1024,128]{0,1:T(8,128)(2,1)S(1)}, u32[]{:S(2)}) copy-start(bf16[1024,128]{0,1:T(8,128)(2,1)S(1)} %fusion.28) | copy-start | bytes 786436
  412.0 4.7 copy-start.52
  418.9 32.8 %copy-start.59 = (f32[32,256]{1,0:T(8,128)S(1)}, f32[32,256]{1,0:T(8,128)}, u32[]{:S(2)}) copy-start(f32[32,256]{1,0:T(8,128)} %get-tuple-element.45) | copy-start | bytes 98308
  418.9 34.3 %copy-start.58 = (f32[32,256]{1,0:T(8,128)S(1)}, f32[32,256]{1,0:T(8,128)}, u32[]{:S(2)}) copy-start(f32[32,256]{1,0:T(8,128)} %get-tuple-element.47) | copy-start | bytes 98308
  454.6 4.7 %copy-start.4 = (bf16[1024,1024]{1,0:T(8,128)(2,1)S(1)}, bf16[1024,1024]{1,0:T(8,128)(2,1)}, u32[]{:S(2)}) copy-start(bf16[1024,1024]{1,0:T(8,128)(2,1)} %copy-done.2) | copy-start | bytes 6291460
  (40 other events, 102.6 us)
